TPU v7x, 128 devices: a whole 4x4x4 slice. The times are simulated.
128 devices in a mesh: patch: 8 (over x, core), proto: 16 (over z, y).
Axes of the slice: x: 4, y: 4, z: 4, core: 2. Of those that a mesh axis runs over, the one named last changes fastest.
Arguments:
- student_feats: bfloat16 [32768, 256], P(('patch', 'proto')), may hold values from -50 to 50
- teacher_feats: bfloat16 [32768, 256], P(('patch', 'proto')), may hold values from -50 to 50
- proto_weight: bfloat16 [256, 131072], P(None, 'proto'), may hold values from -4 to 4
- mask_index: int32 [4096], P(('patch', 'proto')), may hold values from 0 to 255, as said below
- row_weight: bfloat16 [4096], P(('patch', 'proto')), may hold values from 0.5 to 4
Outputs:
- grad_student: float32 [4096, 256], P(('patch', 'proto'))
- grad_proto: float32 [256, 131072], P('patch', 'proto')
- loss: float32 [], replicated
Inputs may be any that keep to these rules, and one draw needn't show every extreme that they name: `mask_index`: entries k * 32 to (k + 1) * 32 - 1 are distinct patch positions of image k, counted from that image's first patch.
All inputs are finite; a program needn't handle non-finite values.
Results may differ from a plain program's by a relative error of at most 0.0057.
Values may be sent and summed in bfloat16 or wider, within the bound.
No kernel may reach another device: no remote copies, remote signals or barrier semaphores. Data moves between devices by JAX's collectives and lax.ppermute only.
A program may use at most 128 MiB of HBM per device.

v0:
```python
import jax
import jax.numpy as jnp
from jax import lax
from jax.sharding import PartitionSpec as P

SK_ITERS = 3
eps = 1e-06
teacher_temp = 0.07
student_temp = 0.1


def unit_rows(values):
    values = values.astype(jnp.float32)
    inverse = lax.rsqrt(jnp.sum(values * values, axis=1) + eps)
    return (values * inverse[:, None], inverse)


def finish(teacher_exp, scale_rows, scale_cols, logits, exp_logits, exp_total, weights):
    codes = teacher_exp * scale_rows[:, None] * scale_cols[None, :]
    student_probs = exp_logits / exp_total[:, None]
    grad_logits = (weights[:, None] * (student_probs - codes)).astype(jnp.bfloat16)
    log_total = jnp.log(exp_total)
    loss_partial = jnp.sum(weights[:, None] * codes * (log_total[:, None] - logits))
    return (grad_logits, loss_partial)


def feature_term(grad_logits, proto_cols):
    return (
        lax.dot_general(
            grad_logits, proto_cols, (((1,), (1,)), ((), ())), preferred_element_type=jnp.float32
        )
        / student_temp
    )


def head_term(student_rows, grad_logits):
    return (
        lax.dot_general(
            student_rows, grad_logits, (((0,), (0,)), ((), ())), preferred_element_type=jnp.float32
        )
        / student_temp
    )


def on_device(student_feats, teacher_feats, proto_weight, mask_index, row_weight):
    highest = lax.Precision.HIGHEST
    unit_student, inverse_student = unit_rows(jnp.take(student_feats, mask_index, axis=0))
    unit_teacher, _ = unit_rows(jnp.take(teacher_feats, mask_index, axis=0))
    own_student = unit_student.astype(jnp.bfloat16)
    own_teacher = unit_teacher.astype(jnp.bfloat16)
    w_float = proto_weight.astype(jnp.float32)
    col_inverse = lax.rsqrt(jnp.sum(w_float * w_float, axis=0) + eps)
    unit_proto = w_float * col_inverse[None, :]
    proto_unit = unit_proto.astype(jnp.bfloat16)
    teacher_rows, student_rows, weights = (
        lax.all_gather(own_teacher, "proto", axis=0, tiled=True),
        lax.all_gather(own_student, "proto", axis=0, tiled=True),
        lax.all_gather(row_weight, "proto", axis=0, tiled=True),
    )
    weights = weights.astype(jnp.float32)
    teacher_exp = jnp.exp(
        jnp.dot(teacher_rows, proto_unit, preferred_element_type=jnp.float32) / teacher_temp
    )
    scale_rows = jnp.ones((teacher_rows.shape[0],), jnp.float32)
    for sweep in range(SK_ITERS):
        col_part = jnp.dot(scale_rows, teacher_exp, precision=highest)
        scale_cols = 1.0 / lax.psum(col_part, "patch")
        row_part = jnp.dot(teacher_exp, scale_cols, precision=highest)
        scale_rows = 1.0 / lax.psum(row_part, "proto")
    logits = jnp.dot(student_rows, proto_unit, preferred_element_type=jnp.float32) / student_temp
    exp_logits = jnp.exp(logits)
    exp_total = lax.psum(jnp.sum(exp_logits, axis=1), "proto")
    grad_logits, loss_partial = finish(
        teacher_exp, scale_rows, scale_cols, logits, exp_logits, exp_total, weights
    )
    feature_grad = lax.psum_scatter(
        feature_term(grad_logits, proto_unit), "proto", scatter_dimension=0, tiled=True
    )
    row_share = proto_unit.shape[0] // lax.axis_size("patch")
    row_offset = lax.axis_index("patch") * row_share
    head_full = lax.psum(head_term(student_rows, grad_logits), "patch")
    inner = jnp.sum(unit_proto * head_full, axis=0)
    whole_grad = col_inverse[None, :] * (head_full - unit_proto * inner[None, :])
    grad_proto = lax.dynamic_slice_in_dim(whole_grad, row_offset, row_share, 0)
    loss_total, weight_total = lax.psum(
        (loss_partial, jnp.sum(row_weight.astype(jnp.float32))), ("patch", "proto")
    )
    grad_student = inverse_student[:, None] * (
        feature_grad - unit_student * jnp.sum(unit_student * feature_grad, axis=1)[:, None]
    )
    return (grad_student, grad_proto, loss_total / weight_total)


def solution(mesh):
    in_specs = (
        P(("patch", "proto"), None),
        P(("patch", "proto"), None),
        P(None, "proto"),
        P(("patch", "proto")),
        P(("patch", "proto")),
    )
    out_specs = (P(("patch", "proto"), None), P("patch", "proto"), P())
    return jax.shard_map(
        on_device, mesh=mesh, in_specs=in_specs, out_specs=out_specs, check_vma=False
    )
```

profile of v0, /device:TPU:1, one launch (start us, length us, event | category | flops | bytes accessed | tf_op | source)
XLA Modules:
  0.0 526.8 jit_solution(3142531026962949100)
XLA Ops:
  8.0 0.0 copy-start
  8.0 0.0 reduce-scatter.2.cloned.1.call-start
  8.1 0.7 compare_select_fusion
  8.7 0.7 compare_and_fusion
  9.4 0.6 gather_fusion
  10.1 1.5 gather_fusion.1
  11.6 0.2 fusion.17
  11.8 0.1 fusion.13
  11.9 20.8 %all_gather.11 = bf16[512,256]{1,0:T(8,128)(2,1)S(1)} all-gather(bf16[32,256]{1,0:T(8,128)(2,1)S(1)} %get-tuple-element.15), channel_id=1, replica_groups=mesh['patch'=8,'proto'=16] {'proto'}, dimensions={0}, use_global_device_ids=true | all-gather | bytes 278528 | tf_op jit(solution)/shard_map/all_gather | solution.py:56
  32.7 3.1 fusion
  35.8 4.5 multiply_exponential_fusion
  40.3 7.9 %fusion.20 = f32[1,8192]{1,0:T(1,128)S(1)} fusion(f32[512,8192]{1,0:T(8,128)S(1)} %multiply_exponential_fusion), kind=kOutput, calls=%fused_computation.41 | convolution fusion | flops 50331648 | bytes 16809984 | tf_op jit(solution)/shard_map/dot_general | solution.py:66
  48.2 26.1 %psum.71 = f32[8192]{0:T(1024)S(1)} all-reduce(f32[8192]{0:T(1024)S(1)} %bitcast.33), channel_id=1, replica_groups=mesh['patch'=8,'proto'=16] {'patch'}, use_global_device_ids=true, to_apply=%region_5.7 | all-reduce | flops 8192 | bytes 65536 | tf_op jit(solution)/shard_map/psum | solution.py:67
  74.4 17.6 %fusion.23 = f32[1,512]{1,0:T(1,128)S(1)} fusion(f32[512,8192]{1,0:T(8,128)} %copy-done.2, f32[8192,1]{0,1:T(1,128)S(1)} %bitcast.29), kind=kOutput, calls=%fused_computation.50 | convolution fusion | flops 50331648 | bytes 16812032 | tf_op jit(solution)/shard_map/dot_general | solution.py:68
  92.0 31.0 %psum.72 = f32[512]{0:T(512)S(1)} all-reduce(f32[512]{0:T(512)S(1)} %bitcast.35), channel_id=1, replica_groups=mesh['patch'=8,'proto'=16] {'proto'}, use_global_device_ids=true, to_apply=%region_6.8 | all-reduce | flops 512 | bytes 4096 | tf_op jit(solution)/shard_map/psum | solution.py:69
  123.0 11.5 %fusion.24 = f32[1,8192]{1,0:T(1,128)S(1)} fusion(f32[512,1]{0,1:T(1,128)S(1)} %bitcast.37, f32[512,8192]{1,0:T(8,128)} %copy-done.2), kind=kOutput, calls=%fused_computation.51 | convolution fusion | flops 50331648 | bytes 16812032 | tf_op jit(solution)/shard_map/dot_general | solution.py:66
  134.5 30.9 %psum.73 = f32[8192]{0:T(1024)S(1)} all-reduce(f32[8192]{0:T(1024)S(1)} %bitcast.30), channel_id=1, replica_groups=mesh['patch'=8,'proto'=16] {'patch'}, use_global_device_ids=true, to_apply=%region_7.9 | all-reduce | flops 8192 | bytes 65536 | tf_op jit(solution)/shard_map/psum | solution.py:67
  165.4 17.6 %fusion.25 = f32[1,512]{1,0:T(1,128)S(1)} fusion(f32[512,8192]{1,0:T(8,128)} %copy-done.2, f32[8192,1]{0,1:T(1,128)S(1)} %bitcast.31), kind=kOutput, calls=%fused_computation.52 | convolution fusion | flops 50331648 | bytes 16812032 | tf_op jit(solution)/shard_map/dot_general | solution.py:68
  183.0 28.5 %psum.74 = f32[512]{0:T(512)S(1)} all-reduce(f32[512]{0:T(512)S(1)} %bitcast.36), channel_id=1, replica_groups=mesh['patch'=8,'proto'=16] {'proto'}, use_global_device_ids=true, to_apply=%region_8.10 | all-reduce | flops 512 | bytes 4096 | tf_op jit(solution)/shard_map/psum | solution.py:69
  211.5 11.5 %fusion.26 = f32[1,8192]{1,0:T(1,128)S(1)} fusion(f32[512,1]{0,1:T(1,128)S(1)} %bitcast.38, f32[512,8192]{1,0:T(8,128)} %copy-done.2), kind=kOutput, calls=%fused_computation.53 | convolution fusion | flops 50331648 | bytes 16812032 | tf_op jit(solution)/shard_map/dot_general | solution.py:66
  223.0 31.0 %psum.75 = f32[8192]{0:T(1024)S(1)} all-reduce(f32[8192]{0:T(1024)S(1)} %bitcast.32), channel_id=1, replica_groups=mesh['patch'=8,'proto'=16] {'patch'}, use_global_device_ids=true, to_apply=%region_9.11 | all-reduce | flops 8192 | bytes 65536 | tf_op jit(solution)/shard_map/psum | solution.py:67
  253.9 0.0 copy-start.3
  254.0 17.8 %fusion.27 = f32[1,512]{1,0:T(1,128)S(1)} fusion(f32[512,8192]{1,0:T(8,128)} %copy-done.2, f32[8192,1]{0,1:T(1,128)S(1)} %bitcast.28), kind=kOutput, calls=%fused_computation.54 | convolution fusion | flops 50331648 | bytes 16812032 | tf_op jit(solution)/shard_map/dot_general | solution.py:68
  271.7 17.8 %all_gather.10 = bf16[512,256]{1,0:T(8,128)(2,1)S(1)} all-gather(bf16[32,256]{1,0:T(8,128)(2,1)S(1)} %get-tuple-element.14), channel_id=1, replica_groups=mesh['patch'=8,'proto'=16] {'proto'}, dimensions={0}, use_global_device_ids=true | all-gather | bytes 278528 | tf_op jit(solution)/shard_map/all_gather | solution.py:57
  289.5 0.0 copy-done.3
  289.5 0.0 copy-start.6
  289.5 7.5 %exponential_reduce_fusion = (f32[512]{0:T(512)S(1)}, f32[512,8192]{1,0:T(8,128)}) fusion(bf16[512,256]{1,0:T(8,128)(2,1)S(1)} %all_gather.10, f32[8192]{0:T(1024)S(1)} %add_rsqrt_fusion, bf16[256,8192]{1,0:T(8,128)(2,1)S(1)} %copy-done.3), kind=kOutput, calls=%fused_computation.6 | convolution fusion | flops 2162163200 | bytes 21268480 | tf_op jit(solution)/shard_map/dot_general | solution.py:70
  297.0 30.9 %all-reduce.2 = (f32[512]{0:T(512)S(1)}, f32[512]{0:T(512)S(1)}) all-reduce(f32[512]{0:T(512)S(1)} %bitcast.34, f32[512]{0:T(512)S(1)} %get-tuple-element.16), channel_id=1, replica_groups=mesh['patch'=8,'proto'=16] {'proto'}, use_global_device_ids=true, to_apply=%region_10.12 | all-reduce | flops 1024 | bytes 8192 | tf_op jit(solution)/shard_map/psum | solution.py:69
  327.9 0.6 dynamic-slice
  329.2 0.0 copy-done.6
  329.2 0.2 dynamic-update-slice
  329.4 29.0 %all-reduce = bf16[512]{0:T(512)(128)(2,1)S(1)} all-reduce(bf16[512]{0:T(512)(128)(2,1)S(1)} %dynamic-update-slice), channel_id=1, replica_groups=mesh['patch'=8,'proto'=16] {'proto'}, use_global_device_ids=true, to_apply=%add | all-reduce | flops 512 | bytes 2048
  358.4 14.4 %multiply_reduce_fusion = (f32[]{:T(128)}, bf16[512,8192]{1,0:T(8,128)(2,1)S(1)}) fusion(f32[512,8192]{1,0:T(8,128)} %copy-done.2, f32[512,8192]{1,0:T(8,128)} %get-tuple-element.17, f32[512]{0:T(512)S(1)} %log.3, f32[8192]{0:T(1024)S(1)} %broadcast_divide_fusion, f32[512]{0:T(512)S(1)} %broadcast_divide_fusion.5, f32[512]{0:T(512)S(1)} %convert_element_type.28, ...), kind=kLoop, calls=%fused_computation.2 | loop fusion | flops 46137344 | bytes 41984004 | tf_op jit(solution)/shard_map/reduce_sum | solution.py:23
  372.9 3.2 copy-done.5
  376.1 3.2 fusion.7
  379.3 0.0 reduce-scatter.2.cloned.1.call-update
  379.3 0.0 all-reduce.5.cloned.1.call-start
  379.4 9.0 %convolution_multiply_fusion = f32[256,8192]{1,0:T(8,128)} fusion(bf16[512,256]{1,0:T(8,128)(2,1)S(1)} %all_gather.10, bf16[512,8192]{1,0:T(8,128)(2,1)} %copy-done.5), kind=kOutput, calls=%fused_computation.7 | convolution fusion | flops 2149580800 | bytes 17039360 | tf_op jit(solution)/shard_map/dot_general | solution.py:38
  388.3 0.0 all-reduce.5.cloned.1.call-update
  388.4 0.6 convert_reduce_fusion
  389.0 85.0 %all-reduce.1 = (f32[]{:T(128)}, f32[]{:T(128)}) all-reduce(f32[]{:T(128)} %get-tuple-element.10, f32[]{:T(128)} %convert_reduce_fusion), channel_id=1, replica_groups=mesh['patch'=8,'proto'=16] {'patch','proto'}, use_global_device_ids=true, to_apply=%region_16.18 | all-reduce | flops 2 | bytes 16 | tf_op jit(solution)/shard_map/psum | solution.py:85
  475.3 0.0 reduce-scatter.2.cloned.1.call-done
  475.3 0.9 fusion.14
  476.2 0.0 copy-start.1
  476.3 1.5 fusion.16
  477.8 32.0 %all-reduce.5.cloned.1.call-done = f32[256,8192]{1,0:T(8,128)} async-done(((f32[256,8192]{1,0:T(8,128)}), f32[256,8192]{1,0:T(8,128)}) %all-reduce.5.cloned.1.call-update) | async-done | bytes 8388624 | tf_op jit(solution)/shard_map/psum | solution.py:81
  509.8 6.0 %multiply_reduce_fusion.1 = (f32[8192]{0:T(1024)S(1)}, f32[256,8192]{1,0:T(8,128)S(1)}) fusion(f32[256,8192]{1,0:T(8,128)} %all-reduce.5.cloned.1.call-done, f32[8192]{0:T(1024)S(1)} %add_rsqrt_fusion, bf16[256,8192]{1,0:T(8,128)(2,1)} %param.9), kind=kLoop, calls=%fused_computation.11 | loop fusion | flops 8380416 | bytes 21037056 | tf_op jit(solution)/shard_map/reduce_sum | solution.py:82
  515.7 2.3 fusion.10
  (21 shorter events, 0.1 us)
Async XLA Ops:
  8.0 1.4 copy-start
  8.0 467.3 %reduce-scatter.2.cloned.1.call-start = ((), (), s32[]{:S(2)}) async-start(), calls=%async_computation.1 | async-start | bytes 557056 | tf_op jit(solution)/shard_map/reduce_scatter | solution.py:76
  40.3 8.0 %copy-start.2 = (f32[512,8192]{1,0:T(8,128)}, f32[512,8192]{1,0:T(8,128)S(1)}, u32[]{:S(2)}) copy-start(f32[512,8192]{1,0:T(8,128)S(1)} %multiply_exponential_fusion) | copy-start | bytes 50331652
  253.9 35.6 %copy-start.3 = (bf16[256,8192]{1,0:T(8,128)(2,1)S(1)}, bf16[256,8192]{1,0:T(8,128)(2,1)}, u32[]{:S(2)}) copy-start(bf16[256,8192]{1,0:T(8,128)(2,1)} %param.9) | copy-start | bytes 12582916
  289.5 38.4 %copy-start.7 = (u32[128]{0:T(128)S(1)}, u32[128]{0:T(128)}, u32[]{:S(2)}) copy-start(u32[128]{0:T(128)} %constant.44) | copy-start | bytes 1540
  289.5 39.6 %copy-start.6 = (bf16[32]{0:T(256)(128)(2,1)S(1)}, bf16[32]{0:T(256)(128)(2,1)}, u32[]{:S(2)}) copy-start(bf16[32]{0:T(256)(128)(2,1)} %param.11) | copy-start | bytes 196
  358.4 17.7 %copy-start.4 = (bf16[256,8192]{1,0:T(8,128)(2,1)S(1)}, bf16[256,8192]{1,0:T(8,128)(2,1)}, u32[]{:S(2)}) copy-start(bf16[256,8192]{1,0:T(8,128)(2,1)} %param.9) | copy-start | bytes 12582916
  372.9 3.2 copy-start.5
  379.3 130.5 %all-reduce.5.cloned.1.call-start = ((), (), s32[]{:S(2)}) async-start(), calls=%async_computation.2 | async-start | bytes 16777216 | tf_op jit(solution)/shard_map/psum | solution.py:81
  476.2 41.8 %copy-start.1 = (bf16[256,256]{1,0:T(8,128)(2,1)S(1)}, bf16[256,256]{1,0:T(8,128)(2,1)}, u32[]{:S(2)}) copy-start(bf16[256,256]{1,0:T(8,128)(2,1)} %param.7) | copy-start | bytes 393220
Sparse Core Ops, SparseCore 0:
  379.4 87.7 reduce-scatter.1
Sparse Core Ops, SparseCore 1:
  388.5 121.3 all-reduce.4
where the time goes:
time: 536 us; the launch traced here: 527 us
  blocking collectives  331 us (62%)
  matrix products  108 us (20%)
  waiting for transfers between devices  32.1 us (6%)
  other arithmetic  30.5 us (6%)
  between operations  18.9 us (4%)
  local copies, waits for them, and re-layouts  6.24 us (1%)
    psum x3, blocking collectives, on_device(): scale_rows = 1.0 / lax.psum(row_part, 'proto')  90.4 us
    psum x3, blocking collectives, on_device(): scale_cols = 1.0 / lax.psum(col_part, 'patch')  88 us
    psum x1, blocking collectives, on_device(): lax.psum((loss_partial, jnp.sum(row_weight.astype(jnp.float32))), ('patch...  85 us
    dot_general x3, matrix products, on_device(): row_part = jnp.dot(teacher_exp, scale_cols, precision=highest)  53 us
    psum x1, waiting for transfers between devices, on_device(): head_full = lax.psum(head_term(student_rows, grad_logits), 'patch')  32 us
    dot_general x3, matrix products, on_device(): col_part = jnp.dot(scale_rows, teacher_exp, precision=highest)  30.8 us
    unnamed x1, blocking collectives  29 us
    all_gather x1, blocking collectives, on_device(): lax.all_gather(own_teacher, 'proto', axis=0, tiled=True)  20.8 us
  transfers between devices with their start and end apart: 2, of which 1 were waited for; matrix products, arithmetic and copies ran while one was open for 2% of the time, Pallas kernels for 0%

commit v1 on v0

--- a/solution.py
+++ b/solution.py
@@ -7,6 +7,32 @@
 eps = 1e-06
 teacher_temp = 0.07
 student_temp = 0.1
+
+
+def edit_routes_all(body, net_axis):
+    mixed_arr, w2, then = (lax.psum(1, axis_name=net_axis), lax.axis_index(net_axis), body.shape[0])
+    piece_next = tall = body
+    x_new = lax.dynamic_update_slice_in_dim(
+        jnp.zeros([m * mixed_arr if ii == 0 else m for ii, m in enumerate(body.shape)], body.dtype),
+        body,
+        w2 * then,
+        axis=0,
+    )
+    for rr in range(1, mixed_arr // 2 + 1):
+        piece_next = lax.ppermute(
+            piece_next, net_axis, perm=[(ii, (ii + 1) % mixed_arr) for ii in range(mixed_arr)]
+        )
+        x_new = lax.dynamic_update_slice_in_dim(
+            x_new, piece_next, (w2 - rr) % mixed_arr * then, axis=0
+        )
+        if 2 * rr < mixed_arr:
+            tall = lax.ppermute(
+                tall, net_axis, perm=[(ii, (ii - 1) % mixed_arr) for ii in range(mixed_arr)]
+            )
+            x_new = lax.dynamic_update_slice_in_dim(
+                x_new, tall, (w2 + rr) % mixed_arr * then, axis=0
+            )
+    return x_new
 
 
 def unit_rows(values):
@@ -53,7 +79,7 @@
     unit_proto = w_float * col_inverse[None, :]
     proto_unit = unit_proto.astype(jnp.bfloat16)
     teacher_rows, student_rows, weights = (
-        lax.all_gather(own_teacher, "proto", axis=0, tiled=True),
+        edit_routes_all(own_teacher, "proto"),
         lax.all_gather(own_student, "proto", axis=0, tiled=True),
         lax.all_gather(row_weight, "proto", axis=0, tiled=True),
     )

time: 536 us -> 568 us (1.060)
  starting transfers between devices: 0.08 us -> 36.5 us
  blocking collectives: 331 us -> 312 us
  waiting for transfers between devices: 32.1 us -> 45 us
    ppermute x0 -> x15, starting transfers between devices: none -> 36.1 us  [the longest x7 33.7 us: edit_routes_all(): lax.ppermute(tall, net_axis, perm=[(ii, (ii - 1) % mixed_arr) for ii in r...]
    all_gather x1 -> x0, blocking collectives: 20.8 us -> none  [on_device(): lax.all_gather(own_teacher, 'proto', axis=0, tiled=True)]
    psum x3, blocking collectives: 88 us -> 104 us  [on_device(): scale_cols = 1.0 / lax.psum(col_part, 'patch')]
    ppermute x0 -> x15, waiting for transfers between devices: none -> 12.9 us  [the longest x8 12.9 us: edit_routes_all(): lax.ppermute(piece_next, net_axis, perm=[(ii, (ii + 1) % mixed_arr) for i...]
    psum x1, blocking collectives: 85 us -> 73.1 us  [on_device(): lax.psum((loss_partial, jnp.sum(row_weight.astype(jnp.float32))), ('patch...]
  transfers between devices with their start and end apart: 2 -> 17, of which waited for: 1 -> 8; matrix products, arithmetic and copies ran while one was open for 2% -> 5% of each run, Pallas kernels for 0% -> 0%
where the time goes in v1:
time: 568 us; the launch traced here: 560 us
  blocking collectives  312 us (55%)
  matrix products  110 us (19%)
  waiting for transfers between devices  45 us (8%)
  starting transfers between devices  36.5 us (6%)
  other arithmetic  30.6 us (5%)
  between operations  19.3 us (3%)
  local copies, waits for them, and re-layouts  6.31 us (1%)
    psum x3, blocking collectives, on_device(): scale_cols = 1.0 / lax.psum(col_part, 'patch')  104 us
    psum x3, blocking collectives, on_device(): scale_rows = 1.0 / lax.psum(row_part, 'proto')  87.4 us
    psum x1, blocking collectives, on_device(): lax.psum((loss_partial, jnp.sum(row_weight.astype(jnp.float32))), ('patch...  73.1 us
    dot_general x3, matrix products, on_device(): row_part = jnp.dot(teacher_exp, scale_cols, precision=highest)  52.8 us
    ppermute x7, starting transfers between devices, edit_routes_all(): lax.ppermute(tall, net_axis, perm=[(ii, (ii - 1) % mixed_arr) for ii in r...  33.7 us
    psum x1, waiting for transfers between devices, on_device(): head_full = lax.psum(head_term(student_rows, grad_logits), 'patch')  32 us
    unnamed x1, blocking collectives  30.9 us
    dot_general x3, matrix products, on_device(): col_part = jnp.dot(scale_rows, teacher_exp, precision=highest)  30.8 us
  transfers between devices with their start and end apart: 17, of which 8 were waited for; matrix products, arithmetic and copies ran while one was open for 5% of the time, Pallas kernels for 0%

profile of v1, /device:TPU:1, one launch (start us, length us, event | category | flops | bytes accessed | tf_op | source)
XLA Modules:
  0.0 559.8 jit_solution(8909379708213916753)
XLA Ops:
  8.1 0.7 compare_select_fusion
  8.8 0.7 compare_and_fusion
  9.4 0.6 gather_fusion
  10.1 1.5 gather_fusion.1
  11.9 2.2 collective-permute-start
  14.1 5.0 collective-permute-start.1
  19.1 3.1 fusion
  22.2 16.5 %all_gather.7 = bf16[512,256]{1,0:T(8,128)(2,1)S(1)} all-gather(bf16[32,256]{1,0:T(8,128)(2,1)S(1)} %fusion.13), channel_id=1, replica_groups=mesh['patch'=8,'proto'=16] {'proto'}, dimensions={0}, use_global_device_ids=true | all-gather | bytes 278528 | tf_op jit(solution)/shard_map/all_gather | solution.py:83
  38.7 10.0 %exponential_reduce_fusion = (f32[512]{0:T(512)S(1)}, f32[512,8192]{1,0:T(8,128)}) fusion(bf16[512,256]{1,0:T(8,128)(2,1)S(1)} %all_gather.7, f32[8192]{0:T(1024)S(1)} %add_rsqrt_fusion, bf16[256,8192]{1,0:T(8,128)(2,1)} %param.9), kind=kOutput, calls=%fused_computation.6 | convolution fusion | flops 2162163200 | bytes 21268480 | tf_op jit(solution)/shard_map/dot_general | solution.py:96
  48.8 0.6 dynamic-slice
  50.3 30.9 %all-reduce = bf16[512]{0:T(512)(128)(2,1)S(1)} all-reduce(bf16[512]{0:T(512)(128)(2,1)S(1)} %dynamic-update-slice), channel_id=1, replica_groups=mesh['patch'=8,'proto'=16] {'proto'}, use_global_device_ids=true, to_apply=%add | all-reduce | flops 512 | bytes 2048
  81.4 4.8 collective-permute-start.3
  86.1 1.1 collective-permute-done.2
  87.3 4.8 collective-permute-start.5
  92.1 1.1 collective-permute-done.4
  93.2 4.8 collective-permute-start.7
  98.0 1.1 collective-permute-done.6
  99.1 4.8 collective-permute-start.9
  103.9 1.1 collective-permute-done.8
  105.0 4.8 collective-permute-start.11
  109.8 1.1 collective-permute-done.10
  110.9 4.8 collective-permute-start.13
  115.7 1.1 collective-permute-done.12
  117.1 6.2 %collective-permute-done.14 = bf16[32,256]{1,0:T(8,128)(2,1)S(1)} collective-permute-done((bf16[32,256]{1,0:T(8,128)(2,1)S(1)}, bf16[32,256]{1,0:T(8,128)(2,1)S(1)}, u32[]{:S(2)}, u32[]{:S(2)}) %collective-permute-start.14) | collective-permute-done | bytes 16416 | tf_op jit(solution)/shard_map/ppermute | solution.py:22
  123.3 4.4 multiply_exponential_fusion
  127.8 7.9 %fusion.20 = f32[1,8192]{1,0:T(1,128)S(1)} fusion(f32[512,8192]{1,0:T(8,128)S(1)} %multiply_exponential_fusion), kind=kOutput, calls=%fused_computation.57 | convolution fusion | flops 50331648 | bytes 16809984 | tf_op jit(solution)/shard_map/dot_general | solution.py:92
  135.7 42.2 %psum.71 = f32[8192]{0:T(1024)S(1)} all-reduce(f32[8192]{0:T(1024)S(1)} %bitcast.33), channel_id=1, replica_groups=mesh['patch'=8,'proto'=16] {'patch'}, use_global_device_ids=true, to_apply=%region_5.7 | all-reduce | flops 8192 | bytes 65536 | tf_op jit(solution)/shard_map/psum | solution.py:93
  177.9 17.6 %fusion.24 = f32[1,512]{1,0:T(1,128)S(1)} fusion(f32[512,8192]{1,0:T(8,128)} %copy-done.2, f32[8192,1]{0,1:T(1,128)S(1)} %bitcast.29), kind=kOutput, calls=%fused_computation.66 | convolution fusion | flops 50331648 | bytes 16812032 | tf_op jit(solution)/shard_map/dot_general | solution.py:94
  195.5 28.5 %psum.72 = f32[512]{0:T(512)S(1)} all-reduce(f32[512]{0:T(512)S(1)} %bitcast.35), channel_id=1, replica_groups=mesh['patch'=8,'proto'=16] {'proto'}, use_global_device_ids=true, to_apply=%region_6.8 | all-reduce | flops 512 | bytes 4096 | tf_op jit(solution)/shard_map/psum | solution.py:95
  224.1 11.5 %fusion.25 = f32[1,8192]{1,0:T(1,128)S(1)} fusion(f32[512,1]{0,1:T(1,128)S(1)} %bitcast.37, f32[512,8192]{1,0:T(8,128)} %copy-done.2), kind=kOutput, calls=%fused_computation.67 | convolution fusion | flops 50331648 | bytes 16812032 | tf_op jit(solution)/shard_map/dot_general | solution.py:92
  235.5 30.7 %psum.73 = f32[8192]{0:T(1024)S(1)} all-reduce(f32[8192]{0:T(1024)S(1)} %bitcast.30), channel_id=1, replica_groups=mesh['patch'=8,'proto'=16] {'patch'}, use_global_device_ids=true, to_apply=%region_7.9 | all-reduce | flops 8192 | bytes 65536 | tf_op jit(solution)/shard_map/psum | solution.py:93
  266.2 17.6 %fusion.26 = f32[1,512]{1,0:T(1,128)S(1)} fusion(f32[512,8192]{1,0:T(8,128)} %copy-done.2, f32[8192,1]{0,1:T(1,128)S(1)} %bitcast.31), kind=kOutput, calls=%fused_computation.68 | convolution fusion | flops 50331648 | bytes 16812032 | tf_op jit(solution)/shard_map/dot_general | solution.py:94
  283.9 30.4 %psum.74 = f32[512]{0:T(512)S(1)} all-reduce(f32[512]{0:T(512)S(1)} %bitcast.36), channel_id=1, replica_groups=mesh['patch'=8,'proto'=16] {'proto'}, use_global_device_ids=true, to_apply=%region_8.10 | all-reduce | flops 512 | bytes 4096 | tf_op jit(solution)/shard_map/psum | solution.py:95
  314.2 11.5 %fusion.27 = f32[1,8192]{1,0:T(1,128)S(1)} fusion(f32[512,1]{0,1:T(1,128)S(1)} %bitcast.38, f32[512,8192]{1,0:T(8,128)} %copy-done.2), kind=kOutput, calls=%fused_computation.69 | convolution fusion | flops 50331648 | bytes 16812032 | tf_op jit(solution)/shard_map/dot_general | solution.py:92
  325.7 30.9 %psum.75 = f32[8192]{0:T(1024)S(1)} all-reduce(f32[8192]{0:T(1024)S(1)} %bitcast.32), channel_id=1, replica_groups=mesh['patch'=8,'proto'=16] {'patch'}, use_global_device_ids=true, to_apply=%region_9.11 | all-reduce | flops 8192 | bytes 65536 | tf_op jit(solution)/shard_map/psum | solution.py:93
  356.6 17.6 %fusion.28 = f32[1,512]{1,0:T(1,128)S(1)} fusion(f32[512,8192]{1,0:T(8,128)} %copy-done.2, f32[8192,1]{0,1:T(1,128)S(1)} %bitcast.28), kind=kOutput, calls=%fused_computation.70 | convolution fusion | flops 50331648 | bytes 16812032 | tf_op jit(solution)/shard_map/dot_general | solution.py:94
  374.2 28.5 %all-reduce.2 = (f32[512]{0:T(512)S(1)}, f32[512]{0:T(512)S(1)}) all-reduce(f32[512]{0:T(512)S(1)} %bitcast.34, f32[512]{0:T(512)S(1)} %get-tuple-element.16), channel_id=1, replica_groups=mesh['patch'=8,'proto'=16] {'proto'}, use_global_device_ids=true, to_apply=%region_10.12 | all-reduce | flops 1024 | bytes 8192 | tf_op jit(solution)/shard_map/psum | solution.py:95
  402.7 14.4 %multiply_reduce_fusion = (f32[]{:T(128)}, bf16[512,8192]{1,0:T(8,128)(2,1)S(1)}) fusion(f32[512,8192]{1,0:T(8,128)} %copy-done.2, f32[512,8192]{1,0:T(8,128)} %get-tuple-element.17, f32[512]{0:T(512)S(1)} %log.3, f32[8192]{0:T(1024)S(1)} %broadcast_divide_fusion, f32[512]{0:T(512)S(1)} %broadcast_divide_fusion.5, f32[512]{0:T(512)S(1)} %convert_element_type.28, ...), kind=kLoop, calls=%fused_computation.2 | loop fusion | flops 46137344 | bytes 41984004 | tf_op jit(solution)/shard_map/reduce_sum | solution.py:49
  417.2 3.2 copy-done.4
  420.4 3.2 fusion.7
  423.9 9.0 %convolution_multiply_fusion = f32[256,8192]{1,0:T(8,128)} fusion(bf16[512,256]{1,0:T(8,128)(2,1)S(1)} %all_gather.7, bf16[512,8192]{1,0:T(8,128)(2,1)} %copy-done.4), kind=kOutput, calls=%fused_computation.7 | convolution fusion | flops 2149580800 | bytes 17039360 | tf_op jit(solution)/shard_map/dot_general | solution.py:64
  432.9 0.6 convert_reduce_fusion
  433.5 73.1 %all-reduce.1 = (f32[]{:T(128)}, f32[]{:T(128)}) all-reduce(f32[]{:T(128)} %get-tuple-element.12, f32[]{:T(128)} %convert_reduce_fusion), channel_id=1, replica_groups=mesh['patch'=8,'proto'=16] {'patch','proto'}, use_global_device_ids=true, to_apply=%region_16.18 | all-reduce | flops 2 | bytes 16 | tf_op jit(solution)/shard_map/psum | solution.py:111
  508.0 0.9 fusion.14
  509.0 1.5 fusion.16
  510.5 32.0 %all-reduce.5.cloned.1.call-done = f32[256,8192]{1,0:T(8,128)} async-done(((f32[256,8192]{1,0:T(8,128)}), f32[256,8192]{1,0:T(8,128)}) %all-reduce.5.cloned.1.call-update) | async-done | bytes 8388624 | tf_op jit(solution)/shard_map/psum | solution.py:107
  542.5 6.0 %multiply_reduce_fusion.1 = (f32[8192]{0:T(1024)S(1)}, f32[256,8192]{1,0:T(8,128)S(1)}) fusion(f32[256,8192]{1,0:T(8,128)} %all-reduce.5.cloned.1.call-done, f32[8192]{0:T(1024)S(1)} %add_rsqrt_fusion, bf16[256,8192]{1,0:T(8,128)(2,1)} %param.9), kind=kLoop, calls=%fused_computation.11 | loop fusion | flops 8380416 | bytes 21037056 | tf_op jit(solution)/shard_map/reduce_sum | solution.py:108
  548.4 2.3 fusion.10
  (66 shorter events, 1.5 us)
Async XLA Ops:
  8.0 1.4 copy-start
  8.0 500.0 %reduce-scatter.2.cloned.1.call-start = ((), (), s32[]{:S(2)}) async-start(), calls=%async_computation.1 | async-start | bytes 557056 | tf_op jit(solution)/shard_map/reduce_scatter | solution.py:102
  11.9 69.4 %collective-permute-start = (bf16[32,256]{1,0:T(8,128)(2,1)S(1)}, bf16[32,256]{1,0:T(8,128)(2,1)S(1)}, u32[]{:S(2)}, u32[]{:S(2)}) collective-permute-start(bf16[32,256]{1,0:T(8,128)(2,1)S(1)} %get-tuple-element.11), channel_id=1, source_target_pairs={{0,1},{1,2},{2,3},{3,4},{4,5},{5,6},{6,7},{7,8},{8,9},{9,10},{10,1... | collective-permute-start | bytes 49160 | tf_op jit(solution)/shard_map/ppermute | solution.py:22
  14.1 67.3 %collective-permute-start.1 = (bf16[32,256]{1,0:T(8,128)(2,1)S(1)}, bf16[32,256]{1,0:T(8,128)(2,1)S(1)}, u32[]{:S(2)}, u32[]{:S(2)}) collective-permute-start(bf16[32,256]{1,0:T(8,128)(2,1)S(1)} %get-tuple-element.11), channel_id=1, source_target_pairs={{0,15},{1,0},{2,1},{3,2},{4,3},{5,4},{6,5},{7,6},{8,7},{9,8},{10,9... | collective-permute-start | bytes 49160 | tf_op jit(solution)/shard_map/ppermute | solution.py:29
  38.7 10.1 %copy-start.6 = (u32[128]{0:T(128)S(1)}, u32[128]{0:T(128)}, u32[]{:S(2)}) copy-start(u32[128]{0:T(128)} %constant.150) | copy-start | bytes 1540
  38.7 11.3 %copy-start.5 = (bf16[32]{0:T(256)(128)(2,1)S(1)}, bf16[32]{0:T(256)(128)(2,1)}, u32[]{:S(2)}) copy-start(bf16[32]{0:T(256)(128)(2,1)} %param.11) | copy-start | bytes 196
  81.3 6.0 %collective-permute-start.2 = (bf16[32,256]{1,0:T(8,128)(2,1)S(1)}, bf16[32,256]{1,0:T(8,128)(2,1)S(1)}, u32[]{:S(2)}, u32[]{:S(2)}) collective-permute-start(bf16[32,256]{1,0:T(8,128)(2,1)S(1)} %collective-permute-done), channel_id=1, source_target_pairs={{0,1},{1,2},{2,3},{3,4},{4,5},{5,6},{6,7},{7,8},{8,9},{9,10},{10,1... | collective-permute-start | bytes 49160 | tf_op jit(solution)/shard_map/ppermute | solution.py:22
  81.4 5.9 %collective-permute-start.3 = (bf16[32,256]{1,0:T(8,128)(2,1)S(1)}, bf16[32,256]{1,0:T(8,128)(2,1)S(1)}, u32[]{:S(2)}, u32[]{:S(2)}) collective-permute-start(bf16[32,256]{1,0:T(8,128)(2,1)S(1)} %collective-permute-done.1), channel_id=1, source_target_pairs={{0,15},{1,0},{2,1},{3,2},{4,3},{5,4},{6,5},{7,6},{8,7},{9,8},{10,9... | collective-permute-start | bytes 49160 | tf_op jit(solution)/shard_map/ppermute | solution.py:29
  87.3 5.9 %collective-permute-start.4 = (bf16[32,256]{1,0:T(8,128)(2,1)S(1)}, bf16[32,256]{1,0:T(8,128)(2,1)S(1)}, u32[]{:S(2)}, u32[]{:S(2)}) collective-permute-start(bf16[32,256]{1,0:T(8,128)(2,1)S(1)} %collective-permute-done.2), channel_id=1, source_target_pairs={{0,1},{1,2},{2,3},{3,4},{4,5},{5,6},{6,7},{7,8},{8,9},{9,10},{10,1... | collective-permute-start | bytes 49160 | tf_op jit(solution)/shard_map/ppermute | solution.py:22
  87.3 5.9 %collective-permute-start.5 = (bf16[32,256]{1,0:T(8,128)(2,1)S(1)}, bf16[32,256]{1,0:T(8,128)(2,1)S(1)}, u32[]{:S(2)}, u32[]{:S(2)}) collective-permute-start(bf16[32,256]{1,0:T(8,128)(2,1)S(1)} %collective-permute-done.3), channel_id=1, source_target_pairs={{0,15},{1,0},{2,1},{3,2},{4,3},{5,4},{6,5},{7,6},{8,7},{9,8},{10,9... | collective-permute-start | bytes 49160 | tf_op jit(solution)/shard_map/ppermute | solution.py:29
  93.2 5.9 %collective-permute-start.6 = (bf16[32,256]{1,0:T(8,128)(2,1)S(1)}, bf16[32,256]{1,0:T(8,128)(2,1)S(1)}, u32[]{:S(2)}, u32[]{:S(2)}) collective-permute-start(bf16[32,256]{1,0:T(8,128)(2,1)S(1)} %collective-permute-done.4), channel_id=1, source_target_pairs={{0,1},{1,2},{2,3},{3,4},{4,5},{5,6},{6,7},{7,8},{8,9},{9,10},{10,1... | collective-permute-start | bytes 49160 | tf_op jit(solution)/shard_map/ppermute | solution.py:22
  93.2 5.9 %collective-permute-start.7 = (bf16[32,256]{1,0:T(8,128)(2,1)S(1)}, bf16[32,256]{1,0:T(8,128)(2,1)S(1)}, u32[]{:S(2)}, u32[]{:S(2)}) collective-permute-start(bf16[32,256]{1,0:T(8,128)(2,1)S(1)} %collective-permute-done.5), channel_id=1, source_target_pairs={{0,15},{1,0},{2,1},{3,2},{4,3},{5,4},{6,5},{7,6},{8,7},{9,8},{10,9... | collective-permute-start | bytes 49160 | tf_op jit(solution)/shard_map/ppermute | solution.py:29
  99.1 5.9 %collective-permute-start.8 = (bf16[32,256]{1,0:T(8,128)(2,1)S(1)}, bf16[32,256]{1,0:T(8,128)(2,1)S(1)}, u32[]{:S(2)}, u32[]{:S(2)}) collective-permute-start(bf16[32,256]{1,0:T(8,128)(2,1)S(1)} %collective-permute-done.6), channel_id=1, source_target_pairs={{0,1},{1,2},{2,3},{3,4},{4,5},{5,6},{6,7},{7,8},{8,9},{9,10},{10,1... | collective-permute-start | bytes 49160 | tf_op jit(solution)/shard_map/ppermute | solution.py:22
  99.1 5.9 %collective-permute-start.9 = (bf16[32,256]{1,0:T(8,128)(2,1)S(1)}, bf16[32,256]{1,0:T(8,128)(2,1)S(1)}, u32[]{:S(2)}, u32[]{:S(2)}) collective-permute-start(bf16[32,256]{1,0:T(8,128)(2,1)S(1)} %collective-permute-done.7), channel_id=1, source_target_pairs={{0,15},{1,0},{2,1},{3,2},{4,3},{5,4},{6,5},{7,6},{8,7},{9,8},{10,9... | collective-permute-start | bytes 49160 | tf_op jit(solution)/shard_map/ppermute | solution.py:29
  105.0 5.9 %collective-permute-start.10 = (bf16[32,256]{1,0:T(8,128)(2,1)S(1)}, bf16[32,256]{1,0:T(8,128)(2,1)S(1)}, u32[]{:S(2)}, u32[]{:S(2)}) collective-permute-start(bf16[32,256]{1,0:T(8,128)(2,1)S(1)} %collective-permute-done.8), channel_id=1, source_target_pairs={{0,1},{1,2},{2,3},{3,4},{4,5},{5,6},{6,7},{7,8},{8,9},{9,10},{10,1... | collective-permute-start | bytes 49160 | tf_op jit(solution)/shard_map/ppermute | solution.py:22
  105.0 5.9 %collective-permute-start.11 = (bf16[32,256]{1,0:T(8,128)(2,1)S(1)}, bf16[32,256]{1,0:T(8,128)(2,1)S(1)}, u32[]{:S(2)}, u32[]{:S(2)}) collective-permute-start(bf16[32,256]{1,0:T(8,128)(2,1)S(1)} %collective-permute-done.9), channel_id=1, source_target_pairs={{0,15},{1,0},{2,1},{3,2},{4,3},{5,4},{6,5},{7,6},{8,7},{9,8},{10,9... | collective-permute-start | bytes 49160 | tf_op jit(solution)/shard_map/ppermute | solution.py:29
  110.9 5.9 %collective-permute-start.12 = (bf16[32,256]{1,0:T(8,128)(2,1)S(1)}, bf16[32,256]{1,0:T(8,128)(2,1)S(1)}, u32[]{:S(2)}, u32[]{:S(2)}) collective-permute-start(bf16[32,256]{1,0:T(8,128)(2,1)S(1)} %collective-permute-done.10), channel_id=1, source_target_pairs={{0,1},{1,2},{2,3},{3,4},{4,5},{5,6},{6,7},{7,8},{8,9},{9,10},{10,1... | collective-permute-start | bytes 49160 | tf_op jit(solution)/shard_map/ppermute | solution.py:22
  110.9 6.1 %collective-permute-start.13 = (bf16[32,256]{1,0:T(8,128)(2,1)S(1)}, bf16[32,256]{1,0:T(8,128)(2,1)S(1)}, u32[]{:S(2)}, u32[]{:S(2)}) collective-permute-start(bf16[32,256]{1,0:T(8,128)(2,1)S(1)} %collective-permute-done.11), channel_id=1, source_target_pairs={{0,15},{1,0},{2,1},{3,2},{4,3},{5,4},{6,5},{7,6},{8,7},{9,8},{10,9... | collective-permute-start | bytes 49160 | tf_op jit(solution)/shard_map/ppermute | solution.py:29
  116.8 6.5 %collective-permute-start.14 = (bf16[32,256]{1,0:T(8,128)(2,1)S(1)}, bf16[32,256]{1,0:T(8,128)(2,1)S(1)}, u32[]{:S(2)}, u32[]{:S(2)}) collective-permute-start(bf16[32,256]{1,0:T(8,128)(2,1)S(1)} %collective-permute-done.12), channel_id=1, source_target_pairs={{0,1},{1,2},{2,3},{3,4},{4,5},{5,6},{6,7},{7,8},{8,9},{9,10},{10,1... | collective-permute-start | bytes 49160 | tf_op jit(solution)/shard_map/ppermute | solution.py:22
  127.7 8.0 %copy-start.2 = (f32[512,8192]{1,0:T(8,128)}, f32[512,8192]{1,0:T(8,128)S(1)}, u32[]{:S(2)}) copy-start(f32[512,8192]{1,0:T(8,128)S(1)} %multiply_exponential_fusion) | copy-start | bytes 50331652
  402.7 17.7 %copy-start.3 = (bf16[256,8192]{1,0:T(8,128)(2,1)S(1)}, bf16[256,8192]{1,0:T(8,128)(2,1)}, u32[]{:S(2)}) copy-start(bf16[256,8192]{1,0:T(8,128)(2,1)} %param.9) | copy-start | bytes 12582916
  417.2 3.2 copy-start.4
  423.6 118.9 %all-reduce.5.cloned.1.call-start = ((), (), s32[]{:S(2)}) async-start(), calls=%async_computation.2 | async-start | bytes 16777216 | tf_op jit(solution)/shard_map/psum | solution.py:107
  508.9 41.8 %copy-start.1 = (bf16[256,256]{1,0:T(8,128)(2,1)S(1)}, bf16[256,256]{1,0:T(8,128)(2,1)}, u32[]{:S(2)}) copy-start(bf16[256,256]{1,0:T(8,128)(2,1)} %param.7) | copy-start | bytes 393220
Sparse Core Ops, SparseCore 0:
  423.7 75.9 reduce-scatter.1
Sparse Core Ops, SparseCore 1:
  433.0 109.4 all-reduce.4
